TPU v7x, 32 devices: a whole 2x2x4 slice. The times are simulated.
32 devices in a mesh: ctx: 8 (over y, x, core), fsdp: 4 (over z).
Axes of the slice: x: 2, y: 2, z: 4, core: 2. Of those that a mesh axis runs over, the one named last changes fastest.
Arguments:
- layer_in: bfloat16 [8, 1024, 1024], P('fsdp', 'ctx'), may hold values from -6 to 6
- cotangent: bfloat16 [8, 1024, 1024], P('fsdp', 'ctx'), may hold values from -6 to 6
- norm1_gain: bfloat16 [1024], P('fsdp'), may hold values from 0.099609375 to 1.8984375
- norm1_shift: bfloat16 [1024], P('fsdp'), may hold values from -3 to 3
- norm2_gain: bfloat16 [1024], P('fsdp'), may hold values from 0.099609375 to 1.8984375
- norm2_shift: bfloat16 [1024], P('fsdp'), may hold values from -3 to 3
- qkv_weight: bfloat16 [1024, 3072], P('fsdp'), may hold values from -4 to 4
- qv_bias: bfloat16 [2048], P('fsdp'), may hold values from -3 to 3
- key_bias: bfloat16 [256], P('fsdp'), may hold values from -3 to 3
- attn_out_weight: bfloat16 [1024, 1024], P('fsdp'), may hold values from -1.5 to 1.5
- attn_out_bias: bfloat16 [1024], P('fsdp'), may hold values from -3 to 3
- ff_in_weight: bfloat16 [1024, 4096], P('fsdp'), may hold values from -0.1875 to 0.1875
- ff_in_bias: bfloat16 [4096], P('fsdp'), may hold values from -3 to 3
- ff_out_weight: bfloat16 [1024, 4096], P('fsdp'), may hold values from -0.09375 to 0.09375
- ff_out_bias: bfloat16 [1024], P('fsdp'), may hold values from -3 to 3
Outputs:
- layer_out: bfloat16 [8, 1024, 1024], P('fsdp', 'ctx')
- input_grad: float32 [8, 1024, 1024], P('fsdp', 'ctx')
- norm1_gain_grad: float32 [1024], P('fsdp')
- norm1_shift_grad: float32 [1024], P('fsdp')
- norm2_gain_grad: float32 [1024], P('fsdp')
- norm2_shift_grad: float32 [1024], P('fsdp')
- qkv_weight_grad: float32 [1024, 3072], P('fsdp')
- qv_bias_grad: float32 [2048], P('fsdp')
- key_bias_grad: float32 [256], P('fsdp')
- attn_out_weight_grad: float32 [1024, 1024], P('fsdp')
- attn_out_bias_grad: float32 [1024], P('fsdp')
- ff_in_weight_grad: float32 [1024, 4096], P('fsdp')
- ff_in_bias_grad: float32 [4096], P('fsdp')
- ff_out_weight_grad: float32 [1024, 4096], P('fsdp')
- ff_out_bias_grad: float32 [1024], P('fsdp')
All inputs are finite; a program needn't handle non-finite values.
Results may differ from a plain program's by a relative error of at most 0.025.
Values may be sent and summed in bfloat16 or wider, within the bound.
A program may use at most 256 MiB of HBM per device.

v0:
```python
import math
import jax
import jax.numpy as jnp
from jax import lax
from jax.sharding import PartitionSpec as P

D = 1024
H = 16
HD = 64
ROT = 16
EPSILON = 1e-05


def layer_norm(inputs, gain_vec, shift_vec):
    average = jnp.mean(inputs, axis=-1, keepdims=True)
    centred = inputs - average
    variance = jnp.mean(centred * centred, axis=-1, keepdims=True)
    inverse = lax.rsqrt(variance + EPSILON)
    normed = centred * inverse
    return (normed * gain_vec + shift_vec, normed, inverse)


def norm_back(upstream, normed, inverse, gain_vec):
    gain_grad = jnp.sum(upstream * normed, axis=0)
    shift_grad = jnp.sum(upstream, axis=0)
    scaled = upstream * gain_vec
    inner = (
        scaled
        - jnp.mean(scaled, axis=-1, keepdims=True)
        - normed * jnp.mean(scaled * normed, axis=-1, keepdims=True)
    )
    return (inverse * inner, gain_grad, shift_grad)


def paired_position(row_ids, half_rows, groups):
    owner = row_ids // (2 * half_rows)
    within = row_ids % (2 * half_rows)
    late = 2 * half_rows * groups - (owner + 2) * half_rows + within
    return jnp.where(within < half_rows, owner * half_rows + within, late)


def rotary_tables(positions):
    halfway = ROT // 2
    freq_steps = jnp.arange(halfway, dtype=jnp.float32)
    frequency = jnp.exp(freq_steps * (-2.0 * math.log(10000.0) / ROT))
    theta = positions.astype(jnp.float32)[:, None] * frequency[None, :]
    return (jnp.cos(theta)[:, None, :], jnp.sin(theta)[:, None, :])


def rotate(inputs, cosine, sine):
    halfway = ROT // 2
    first = inputs[..., :halfway]
    second = inputs[..., halfway:ROT]
    return jnp.concatenate(
        [first * cosine - second * sine, second * cosine + first * sine, inputs[..., ROT:]], axis=-1
    )


def rotate_back(upstream, cosine, sine):
    halfway = ROT // 2
    first = upstream[..., :halfway]
    second = upstream[..., halfway:ROT]
    return jnp.concatenate(
        [first * cosine + second * sine, second * cosine - first * sine, upstream[..., ROT:]],
        axis=-1,
    )


def gelu_parts(inputs):
    cumulative = 0.5 * (1.0 + lax.erf(inputs * (1.0 / math.sqrt(2.0))))
    density = jnp.exp(-0.5 * inputs * inputs) * (1.0 / math.sqrt(2.0 * math.pi))
    return (inputs * cumulative, cumulative + inputs * density)


def contract_rows(left, right):
    return lax.dot_general(
        left, right, (((0,), (0,)), ((), ())), preferred_element_type=jnp.float32
    )


def contract_cols(left, right):
    return lax.dot_general(
        left, right, (((1,), (1,)), ((), ())), preferred_element_type=jnp.float32
    )


def blocked(matrix, blocks, key_block):
    seq_count = matrix.shape[0]
    return matrix.reshape(seq_count, blocks, key_block, H, HD).transpose(1, 0, 2, 3, 4)


def per_device(
    layer_in,
    cotangent,
    norm1_gain,
    norm1_shift,
    norm2_gain,
    norm2_shift,
    qkv_weight,
    qv_bias,
    key_bias,
    attn_out_weight,
    attn_out_bias,
    ff_in_weight,
    ff_in_bias,
    ff_out_weight,
    ff_out_bias,
):
    ctx_count = lax.axis_size("ctx")
    shard_count = lax.axis_size("fsdp")
    ctx_place = lax.axis_index("ctx")
    shard_place = lax.axis_index("fsdp")
    seq_count = layer_in.shape[0]
    tokens = layer_in.shape[1]
    half_rows = tokens // 2
    row_total = seq_count * tokens
    inputs_f = layer_in.reshape(row_total, D).astype(jnp.float32)
    upstream = cotangent.reshape(row_total, D)
    upstream_f = upstream.astype(jnp.float32)
    gathered = (
        lax.all_gather(norm1_gain, "fsdp", axis=0, tiled=True),
        lax.all_gather(norm1_shift, "fsdp", axis=0, tiled=True),
        lax.all_gather(norm2_gain, "fsdp", axis=0, tiled=True),
        lax.all_gather(norm2_shift, "fsdp", axis=0, tiled=True),
        lax.all_gather(qv_bias, "fsdp", axis=0, tiled=True),
        lax.all_gather(key_bias, "fsdp", axis=0, tiled=True),
        lax.all_gather(attn_out_bias, "fsdp", axis=0, tiled=True),
        lax.all_gather(ff_in_bias, "fsdp", axis=0, tiled=True),
        lax.all_gather(ff_out_bias, "fsdp", axis=0, tiled=True),
    )
    (
        gain_one,
        shift_one,
        gain_two,
        shift_two,
        query_value_bias,
        rotary_bias,
        attn_bias,
        ff_bias,
        out_bias,
    ) = [piece.astype(jnp.float32) for piece in gathered]
    key_full = jnp.concatenate(
        [rotary_bias.reshape(H, ROT), jnp.zeros((H, HD - ROT), jnp.float32)], axis=1
    ).reshape(D)
    in_bias = jnp.concatenate([query_value_bias[:D], key_full, query_value_bias[D:]])
    qkv_full, ff_in_full, attn_out_full, ff_out_full = (
        lax.all_gather(qkv_weight, "fsdp", axis=0, tiled=True),
        lax.all_gather(ff_in_weight, "fsdp", axis=0, tiled=True),
        lax.all_gather(attn_out_weight, "fsdp", axis=0, tiled=True),
        lax.all_gather(ff_out_weight, "fsdp", axis=0, tiled=True),
    )
    query_pos = paired_position(
        jnp.arange(tokens, dtype=jnp.int32) + ctx_place * tokens, half_rows, ctx_count
    )
    cosine, sine = rotary_tables(query_pos)
    normed_one, unit_one, inverse_one = layer_norm(inputs_f, gain_one, shift_one)
    normed_two, unit_two, inverse_two = layer_norm(inputs_f, gain_two, shift_two)
    one_b = normed_one.astype(jnp.bfloat16)
    two_b = normed_two.astype(jnp.bfloat16)
    projected = jnp.dot(one_b, qkv_full, preferred_element_type=jnp.float32) + in_bias
    ff_pre = jnp.dot(two_b, ff_in_full, preferred_element_type=jnp.float32) + ff_bias
    query_b = rotate(projected[:, :D].reshape(seq_count, tokens, H, HD), cosine, sine).astype(
        jnp.bfloat16
    )
    keys_b = rotate(projected[:, D : 2 * D].reshape(seq_count, tokens, H, HD), cosine, sine).astype(
        jnp.bfloat16
    )
    values_b = projected[:, 2 * D :].astype(jnp.bfloat16).reshape(seq_count, tokens, D)
    all_keys, all_values = (
        lax.all_gather(keys_b.reshape(seq_count, tokens, D), "ctx", axis=1, tiled=True),
        lax.all_gather(values_b, "ctx", axis=1, tiled=True),
    )
    key_total = all_keys.shape[1]
    key_block = math.gcd(key_total, 512)
    blocks = key_total // key_block
    key_pos = paired_position(jnp.arange(key_total, dtype=jnp.int32), half_rows, ctx_count).reshape(
        blocks, key_block
    )
    keys_blocked = blocked(all_keys, blocks, key_block)
    values_blocked = blocked(all_values, blocks, key_block)

    def block_scores(key_piece, pos_piece):
        scores = (
            jnp.einsum("sqhd,skhd->shqk", query_b, key_piece, preferred_element_type=jnp.float32)
            * 0.125
        )
        allowed = pos_piece[None, None, None, :] <= query_pos[None, None, :, None]
        return (jnp.where(allowed, scores, -1e30), allowed)

    def first_pass(state, inputs):
        highest, total = state
        scores, allowed = block_scores(inputs[0], inputs[1])
        new_high = jnp.maximum(highest, jnp.max(scores, axis=-1))
        total = total * jnp.exp(highest - new_high) + jnp.sum(
            jnp.exp(scores - new_high[..., None]), axis=-1
        )
        return ((new_high, total), None)

    start_state = (
        jnp.full((seq_count, H, tokens), -1e30, jnp.float32),
        jnp.zeros((seq_count, H, tokens), jnp.float32),
    )
    (highest, total), unused = lax.scan(first_pass, start_state, (keys_blocked, key_pos))
    log_total = highest + jnp.log(total)

    def second_pass(mixed, inputs):
        scores, allowed = block_scores(inputs[0], inputs[2])
        weights = jnp.where(allowed, jnp.exp(scores - log_total[..., None]), 0.0).astype(
            jnp.bfloat16
        )
        return (
            mixed
            + jnp.einsum("shqk,skhd->sqhd", weights, inputs[1], preferred_element_type=jnp.float32),
            None,
        )

    mixed, unused = lax.scan(
        second_pass,
        jnp.zeros((seq_count, tokens, H, HD), jnp.float32),
        (keys_blocked, values_blocked, key_pos),
    )
    attn_b = mixed.reshape(row_total, D).astype(jnp.bfloat16)
    activation, slope = gelu_parts(ff_pre)
    gelu_b = activation.astype(jnp.bfloat16)
    act_cat = jnp.concatenate([attn_b, gelu_b], axis=1)
    out_cat = jnp.concatenate([attn_out_full, ff_out_full], axis=1)
    mixture = contract_cols(act_cat, out_cat)
    layer_out = (inputs_f + mixture + attn_bias + out_bias).astype(jnp.bfloat16)
    back_cat = jnp.dot(upstream, out_cat, preferred_element_type=jnp.float32)
    dout_b = back_cat[:, :D].astype(jnp.bfloat16).reshape(seq_count, tokens, H, HD)
    dpre = back_cat[:, D:] * slope
    dpre_b = dpre.astype(jnp.bfloat16)
    delta = jnp.sum(
        dout_b.astype(jnp.float32) * attn_b.astype(jnp.float32).reshape(seq_count, tokens, H, HD),
        axis=-1,
    ).transpose(0, 2, 1)

    def query_side(dquery, inputs):
        key_piece, value_piece, pos_piece = inputs
        scores, allowed = block_scores(key_piece, pos_piece)
        probs = jnp.where(allowed, jnp.exp(scores - log_total[..., None]), 0.0)
        dprobs = jnp.einsum(
            "sqhd,skhd->shqk", dout_b, value_piece, preferred_element_type=jnp.float32
        )
        dscores = (probs * (dprobs - delta[..., None])).astype(jnp.bfloat16)
        dquery = (
            dquery
            + jnp.einsum("shqk,skhd->sqhd", dscores, key_piece, preferred_element_type=jnp.float32)
            * 0.125
        )
        return (dquery, (probs, dscores))

    zero_query = jnp.zeros((seq_count, tokens, H, HD), jnp.float32)

    def dquery_pass(dquery, inputs):
        dquery, unused_pair = query_side(dquery, inputs)
        return (dquery, None)

    dquery, unused = lax.scan(dquery_pass, zero_query, (keys_blocked, values_blocked, key_pos))
    all_query, all_dout = (
        lax.all_gather(query_b.reshape(seq_count, tokens, D), "ctx", axis=1, tiled=True),
        lax.all_gather(dout_b.reshape(seq_count, tokens, D), "ctx", axis=1, tiled=True),
    )
    all_lse, all_delta = (
        lax.all_gather(log_total, "ctx", axis=2, tiled=True),
        lax.all_gather(delta, "ctx", axis=2, tiled=True),
    )
    own_values = values_b.reshape(seq_count, tokens, H, HD)
    query_blocked = blocked(all_query, blocks, key_block)
    dout_blocked = blocked(all_dout, blocks, key_block)
    lse_blocked = all_lse.reshape(seq_count, H, blocks, key_block).transpose(2, 0, 1, 3)
    delta_blocked = all_delta.reshape(seq_count, H, blocks, key_block).transpose(2, 0, 1, 3)

    def key_pass(sums, inputs):
        key_sum, value_sum = sums
        rows_q, rows_do, rows_lse, rows_delta, pos_q = inputs
        scores = (
            jnp.einsum("sqhd,skhd->shqk", rows_q, keys_b, preferred_element_type=jnp.float32)
            * 0.125
        )
        allowed = query_pos[None, None, None, :] <= pos_q[None, None, :, None]
        probs = jnp.where(
            allowed, jnp.exp(jnp.where(allowed, scores, -1e30) - rows_lse[..., None]), 0.0
        )
        dprobs = jnp.einsum(
            "sqhd,skhd->shqk", rows_do, own_values, preferred_element_type=jnp.float32
        )
        dscores = (probs * (dprobs - rows_delta[..., None])).astype(jnp.bfloat16)
        key_sum = (
            key_sum
            + jnp.einsum("shqk,sqhd->skhd", dscores, rows_q, preferred_element_type=jnp.float32)
            * 0.125
        )
        value_sum = value_sum + jnp.einsum(
            "shqk,sqhd->skhd",
            probs.astype(jnp.bfloat16),
            rows_do,
            preferred_element_type=jnp.float32,
        )
        return ((key_sum, value_sum), None)

    (dkey_own, dvalue_own), unused = lax.scan(
        key_pass,
        (zero_query, zero_query),
        (query_blocked, dout_blocked, lse_blocked, delta_blocked, key_pos),
    )
    dquery_pre = rotate_back(dquery, cosine, sine).reshape(row_total, D)
    dkey_pre = rotate_back(dkey_own, cosine, sine)
    dvalue_rows = dvalue_own.reshape(row_total, D)
    dproj = jnp.concatenate([dquery_pre, dkey_pre.reshape(row_total, D), dvalue_rows], axis=1)
    dproj_b = dproj.astype(jnp.bfloat16)
    dnormed_one = contract_cols(dproj_b, qkv_full)
    dnormed_two = contract_cols(dpre_b, ff_in_full)
    dinput_one, gain_grad_one, shift_grad_one = norm_back(
        dnormed_one, unit_one, inverse_one, gain_one
    )
    dinput_two, gain_grad_two, shift_grad_two = norm_back(
        dnormed_two, unit_two, inverse_two, gain_two
    )
    input_grad = (upstream_f + dinput_one + dinput_two).reshape(seq_count, tokens, D)

    def make_terms(cot_left, one_left, two_left):

        def out_term(start, count):
            return contract_rows(cot_left, act_cat)

        def in_term(start, count):
            return jnp.concatenate(
                [contract_rows(one_left, dproj_b), contract_rows(two_left, dpre_b)], axis=1
            )

        return (out_term, in_term)

    row_count = D // shard_count
    out_term, in_term = make_terms(upstream, one_b, two_b)
    out_part = lax.psum_scatter(
        out_term(jnp.int32(0), row_count * lax.axis_size("fsdp")).astype(jnp.bfloat16),
        "fsdp",
        scatter_dimension=0,
        tiled=True,
    ).astype(jnp.float32)
    in_part = lax.psum_scatter(
        in_term(jnp.int32(0), row_count * lax.axis_size("fsdp")).astype(jnp.bfloat16),
        "fsdp",
        scatter_dimension=0,
        tiled=True,
    ).astype(jnp.float32)
    out_part, in_part = (
        lax.psum(out_part.astype(jnp.bfloat16), "ctx").astype(jnp.float32),
        lax.psum(in_part.astype(jnp.bfloat16), "ctx").astype(jnp.float32),
    )
    qv_grad = jnp.concatenate([jnp.sum(dquery_pre, axis=0), jnp.sum(dvalue_rows, axis=0)])
    rotary_grad = jnp.sum(dkey_pre[..., :ROT], axis=(0, 1)).reshape(H * ROT)
    cot_grad = jnp.sum(upstream_f, axis=0)
    ff_bias_grad = jnp.sum(dpre, axis=0)
    summed = lax.psum(
        (
            gain_grad_one,
            shift_grad_one,
            gain_grad_two,
            shift_grad_two,
            qv_grad,
            rotary_grad,
            cot_grad,
            ff_bias_grad,
        ),
        ("ctx", "fsdp"),
    )

    def own_share(vector):
        width = vector.shape[0] // shard_count
        return lax.dynamic_slice_in_dim(vector, shard_place * width, width, 0)

    shares = [own_share(vector) for vector in summed]
    return (
        layer_out.reshape(seq_count, tokens, D),
        input_grad,
        shares[0],
        shares[1],
        shares[2],
        shares[3],
        in_part[:, : 3 * D],
        shares[4],
        shares[5],
        out_part[:, :D],
        shares[6],
        in_part[:, 3 * D :],
        shares[7],
        out_part[:, D:],
        shares[6],
    )


def solution(mesh):
    placed = (
        P("fsdp", "ctx", None),
        P("fsdp", "ctx", None),
        P("fsdp"),
        P("fsdp"),
        P("fsdp"),
        P("fsdp"),
        P("fsdp", None),
        P("fsdp"),
        P("fsdp"),
        P("fsdp", None),
        P("fsdp"),
        P("fsdp", None),
        P("fsdp"),
        P("fsdp", None),
        P("fsdp"),
    )
    return jax.shard_map(
        per_device,
        mesh=mesh,
        in_specs=placed,
        out_specs=(
            P("fsdp", "ctx", None),
            P("fsdp", "ctx", None),
            P("fsdp"),
            P("fsdp"),
            P("fsdp"),
            P("fsdp"),
            P("fsdp", None),
            P("fsdp"),
            P("fsdp"),
            P("fsdp", None),
            P("fsdp"),
            P("fsdp", None),
            P("fsdp"),
            P("fsdp", None),
            P("fsdp"),
        ),
        check_vma=False,
    )
```

profile of v0, /device:TPU:0, one launch (start us, length us, event | category | flops | bytes accessed | tf_op | source)
XLA Modules:
  0.0 1189.8 jit_solution(6554706821487634734)
XLA Ops:
  10.1 12.7 %all-gather.1 = bf16[4,1,256]{2,1,0:T(2,128)(2,1)S(1)} all-gather(bf16[1,1,256]{2,1,0:T(2,128)(2,1)S(1)} %reshape.446), channel_id=1, replica_groups=mesh['ctx'=8,'fsdp'=4] {'fsdp'}, dimensions={0}, use_global_device_ids=true | all-gather | bytes 2560 | tf_op jit(solution)/shard_map/all_gather | solution.py:122
  22.8 8.1 all-gather
  30.9 14.0 %all-gather.4 = bf16[4,1,256]{2,1,0:T(2,128)(2,1)S(1)} all-gather(bf16[1,1,256]{2,1,0:T(2,128)(2,1)S(1)} %reshape.452), channel_id=1, replica_groups=mesh['ctx'=8,'fsdp'=4] {'fsdp'}, dimensions={0}, use_global_device_ids=true | all-gather | bytes 2560 | tf_op jit(solution)/shard_map/all_gather | solution.py:124
  45.0 8.7 all-gather.3
  55.2 10.4 all-reduce.1
  65.7 22.4 %all-gather.2 = bf16[4,1,512]{2,1,0:T(2,128)(2,1)S(1)} all-gather(bf16[1,1,512]{2,1,0:T(2,128)(2,1)S(1)} %reshape.448), channel_id=1, replica_groups=mesh['ctx'=8,'fsdp'=4] {'fsdp'}, dimensions={0}, use_global_device_ids=true | all-gather | bytes 5120 | tf_op jit(solution)/shard_map/all_gather | solution.py:125
  90.4 37.9 %all-gather.16.cloned.1.call-done = bf16[1024,3072]{1,0:T(8,128)(2,1)} async-done(((bf16[256,3072]{1,0:T(8,128)(2,1)}), bf16[1024,3072]{1,0:T(8,128)(2,1)}) %all-gather.16.cloned.1.call-update) | async-done | bytes 6291472 | tf_op jit(solution)/shard_map/all_gather | solution.py:147
  128.3 4.6 convolution_add_fusion.1
  135.8 2.9 fusion.171
  150.8 12.4 %all_gather.67 = bf16[4096]{0:T(1024)(128)(2,1)S(1)} all-gather(bf16[1024]{0:T(1024)(128)(2,1)S(1)} %copy-done.39), channel_id=1, replica_groups=mesh['ctx'=8,'fsdp'=4] {'fsdp'}, dimensions={0}, use_global_device_ids=true | all-gather | bytes 10240 | tf_op jit(solution)/shard_map/all_gather | solution.py:128
  163.2 10.6 all-gather.24.cloned.1.call-done
  173.8 3.1 constant_dynamic-update-slice_fusion.1
  177.0 146.9 %all-gather.26.cloned.1.call-done = bf16[1024,4096]{1,0:T(8,128)(2,1)} async-done(((bf16[256,4096]{1,0:T(8,128)(2,1)}), bf16[1024,4096]{1,0:T(8,128)(2,1)}) %all-gather.26.cloned.1.call-update) | async-done | bytes 8388624 | tf_op jit(solution)/shard_map/all_gather | solution.py:150
  323.8 8.3 constant_dynamic-update-slice_fusion
  332.1 6.5 convolution_bitcast_fusion
  342.8 130.3 %all-gather.22.cloned.1.call-done = bf16[1024,4096]{1,0:T(8,128)(2,1)} async-done(((bf16[256,4096]{1,0:T(8,128)(2,1)}), bf16[1024,4096]{1,0:T(8,128)(2,1)}) %all-gather.22.cloned.1.call-update) | async-done | bytes 8388624 | tf_op jit(solution)/shard_map/all_gather | solution.py:148
  473.1 9.2 fusion.167
  482.3 28.6 %all-gather.18.cloned.1.call-done = bf16[2,1024,1024]{1,2,0:T(8,128)(2,1)} async-done(((bf16[2,128,1024]{1,2,0:T(8,128)(2,1)}), bf16[2,1024,1024]{1,2,0:T(8,128)(2,1)}) %all-gather.18.cloned.1.call-update) | async-done | bytes 4194320 | tf_op jit(solution)/shard_map/all_gather | solution.py:171
  511.0 7.8 reshape.422
  518.8 5.4 copy.89
  524.2 25.9 %all-gather.20.cloned.1.call-done = bf16[2,1024,1024]{1,2,0:T(8,128)(2,1)} async-done(((bf16[2,128,1024]{1,2,0:T(8,128)(2,1)}), bf16[2,1024,1024]{1,2,0:T(8,128)(2,1)}) %all-gather.20.cloned.1.call-update) | async-done | bytes 4194320 | tf_op jit(solution)/shard_map/all_gather | solution.py:170
  550.1 7.8 reshape.424
  557.9 5.6 copy.90
  563.5 24.2 %while.48 = (s32[]{:T(128)}, f32[2,16,128]{2,1,0:T(8,128)S(1)}, f32[2,16,128]{2,1,0:T(8,128)S(1)}, s32[2,512]{1,0:T(2,128)S(1)}, bf16[2,2,512,16,64]{2,4,3,1,0:T...) while((s32[]{:T(128)}, f32[2,16,128]{2,1,0:T(8,128)S(1)}, ...), condition=%wide.region_5.6_spmd.clone, body=%wide.region_2.5_spmd.clone.sunk | while | flops 283205120 | bytes 19815548 | solution.py:203
  563.6 6.7 fusion.223
  570.3 5.2 exponential_reduce_fusion.2
  575.8 6.7 fusion.223
  582.4 5.2 exponential_reduce_fusion.2
  587.7 13.5 %while.49 = (s32[]{:T(128)}, f32[2,128,16,64]{1,3,2,0:T(8,128)}, bf16[2,2,512,16,64]{2,4,3,1,0:T(8,128)(2,1)}, s32[2,512]{1,0:T(2,128)S(1)}, bf16[2,2,512,16,64]...) while((s32[]{:T(128)}, f32[2,128,16,64]{1,3,2,0:T(8,128)}, ...), condition=%wide.region_7.8_spmd.clone, body=%wide.region_6.7_spmd.clone.sunk | while | flops 547950080 | bytes 6972030 | solution.py:217
  587.9 6.2 fusion.229
  594.2 6.4 fusion.229
  604.8 7.2 convert_bitcast_fusion
  613.9 2.8 copy.113
  617.6 7.4 convolution_convert_fusion
  625.0 30.8 %while.50 = (s32[]{:T(128)}, f32[2,128,16,64]{1,3,2,0:T(8,128)S(1)}, bf16[2,2,512,16,64]{2,4,3,1,0:T(8,128)(2,1)}, s32[2,512]{1,0:T(2,128)S(1)}, bf16[2,128,16,6...) while((s32[]{:T(128)}, ...), condition=%wide.region_10.11_spmd.clone, body=%wide.region_9.10_spmd.clone.sunk | while | flops 820841984 | bytes 26387088 | solution.py:259
  625.2 6.2 fusion.236
  631.6 8.8 fusion.237
  640.5 6.2 fusion.236
  646.9 8.9 fusion.237
  657.7 7.8 reshape.430
  665.5 5.2 copy.109
  670.7 9.3 all_gather.73
  680.1 8.4 all_gather.75
  688.6 8.0 reshape.432
  696.7 5.2 copy.112
  701.9 48.0 %while.51 = (s32[]{:T(128)}, f32[2,128,16,64]{1,3,2,0:T(8,128)S(1)}, f32[2,128,16,64]{1,3,2,0:T(8,128)}, bf16[2,2,512,16,64]{2,4,3,1,0:T(8,128)(2,1)}, s32[2,512...) while((s32[]{:T(128)}, ...), condition=%wide.region_12.13_spmd.clone, body=%wide.region_11.12_spmd.clone.sunk | while | flops 1100287488 | bytes 39723684 | solution.py:302
  701.9 6.3 fusion.245
  708.5 11.0 fusion.246
  719.5 6.3 fusion.247
  725.8 6.3 fusion.245
  732.4 10.7 fusion.246
  743.1 6.5 fusion.247
  758.9 10.5 pad_maximum_fusion
  770.0 11.4 all-gather.6
  782.0 9.6 all-gather.5
  792.9 16.3 %reduce-scatter.5.cloned.1.call-done = bf16[256,5120]{0,1:T(8,128)(2,1)} async-done(((bf16[1024,5120]{0,1:T(8,128)(2,1)}), bf16[256,5120]{0,1:T(8,128)(2,1)}) %reduce-scatter.5.cloned.1.call-update) | async-done | bytes 2621456 | tf_op jit(solution)/shard_map/reduce_scatter | solution.py:336
  809.1 248.9 %reduce-scatter.3.cloned.1.call-done = bf16[256,7168]{1,0:T(8,128)(2,1)} async-done(((bf16[1024,7168]{1,0:T(8,128)(2,1)}), bf16[256,7168]{1,0:T(8,128)(2,1)}) %reduce-scatter.3.cloned.1.call-update) | async-done | bytes 3670032 | tf_op jit(solution)/shard_map/reduce_scatter | solution.py:342
  1058.2 7.5 fusion.159
  1066.5 3.8 fusion.156
  1073.2 7.1 multiply_reduce_fusion.1
  1080.3 42.5 %all-reduce.2 = (f32[1024]{0:T(1024)S(1)}, f32[1024]{0:T(1024)S(1)}, f32[1024]{0:T(1024)S(1)}, f32[1024]{0:T(1024)S(1)}, f32[2048]{0:T(1024)S(1)}, /*index=5*/f3...) all-reduce(f32[1024]{0:T(1024)S(1)} %get-tuple-element.477, ...), channel_id=1, replica_groups=mesh['ctx'=8,'fsdp'=4] {'ctx','fsdp'}, use_global_device_ids=true, to_apply=%region_18.19 | all-reduce | flops 11520 | bytes 92160 | tf_op jit(solution)/shard_map/psum | solution.py:356
  1130.1 37.1 %all-reduce.6.cloned.1.call-done = (bf16[256,7168]{1,0:T(8,128)(2,1)}, bf16[256,5120]{0,1:T(8,128)(2,1)}) async-done(((bf16[256,7168]{1,0:T(8,128)(2,1)}, bf16[256,5120]{0,1:T(8,128)(2,1)}), (bf16[256,7168]{1,0:T(8,128)(2,1)}, bf16[256,5120]{0,1:T(8,128)(2,1)})) %all-reduce.6.cloned.1.call-update) | async-done | bytes 6291472 | tf_op jit(solution)/shard_map/psum | solution.py:350
  1167.2 3.6 slice.117
  1177.0 5.6 copy.122
  (278 shorter events, 64.0 us)
Async XLA Ops:
  7.2 46.5 %copy-start.48 = (u32[32]{0:T(128)S(1)}, u32[32]{0:T(128)}, u32[]{:S(2)}) copy-start(u32[32]{0:T(128)} %constant.185) | copy-start | bytes 388
  7.2 2.9 copy-start.41
  7.2 15.6 %copy-start.42 = (bf16[256]{0:T(256)(128)(2,1)S(1)}, bf16[256]{0:T(256)(128)(2,1)}, u32[]{:S(2)}) copy-start(bf16[256]{0:T(256)(128)(2,1)} %param.25) | copy-start | bytes 1540
  7.2 23.7 %copy-start.43 = (bf16[256]{0:T(256)(128)(2,1)S(1)}, bf16[256]{0:T(256)(128)(2,1)}, u32[]{:S(2)}) copy-start(bf16[256]{0:T(256)(128)(2,1)} %param.28) | copy-start | bytes 1540
  7.2 37.7 %copy-start.44 = (bf16[256]{0:T(256)(128)(2,1)S(1)}, bf16[256]{0:T(256)(128)(2,1)}, u32[]{:S(2)}) copy-start(bf16[256]{0:T(256)(128)(2,1)} %param.27) | copy-start | bytes 1540
  7.2 46.4 %copy-start.40 = (bf16[512]{0:T(512)(128)(2,1)S(1)}, bf16[512]{0:T(512)(128)(2,1)}, u32[]{:S(2)}) copy-start(bf16[512]{0:T(512)(128)(2,1)} %param.30) | copy-start | bytes 3076
  7.2 47.7 %copy-start.45 = (bf16[64]{0:T(256)(128)(2,1)S(1)}, bf16[64]{0:T(256)(128)(2,1)}, u32[]{:S(2)}) copy-start(bf16[64]{0:T(256)(128)(2,1)} %param.31) | copy-start | bytes 388
  7.3 80.9 %copy-start.3 = (bf16[2,128,1024]{2,1,0:T(8,128)(2,1)S(1)}, bf16[2,128,1024]{2,1,0:T(8,128)(2,1)}, u32[]{:S(2)}) copy-start(bf16[2,128,1024]{2,1,0:T(8,128)(2,1)} %param.23) | copy-start | bytes 1572868
  7.3 121.0 %all-gather.16.cloned.1.call-start = ((), (), s32[]{:S(2)}) async-start(), calls=%async_computation.2 | async-start | bytes 7864320 | tf_op jit(solution)/shard_map/all_gather | solution.py:147
  8.0 165.8 %all-gather.24.cloned.1.call-start = ((), (), s32[]{:S(2)}) async-start(), calls=%async_computation.6 | async-start | bytes 2621440 | tf_op jit(solution)/shard_map/all_gather | solution.py:149
  8.7 315.1 %all-gather.26.cloned.1.call-start = ((), (), s32[]{:S(2)}) async-start(), calls=%async_computation.7 | async-start | bytes 10485760 | tf_op jit(solution)/shard_map/all_gather | solution.py:150
  9.5 463.6 %all-gather.22.cloned.1.call-start = ((), (), s32[]{:S(2)}) async-start(), calls=%async_computation.5 | async-start | bytes 10485760 | tf_op jit(solution)/shard_map/all_gather | solution.py:148
  10.1 500.9 %all-gather.18.cloned.1.call-start = ((), (), s32[]{:S(2)}) async-start(), calls=%async_computation.3 | async-start | bytes 4718592 | tf_op jit(solution)/shard_map/all_gather | solution.py:171
  30.9 102.0 %copy-start.22 = (f32[4,1,256]{2,1,0:T(1,128)}, f32[4,1,256]{2,1,0:T(1,128)S(1)}, u32[]{:S(2)}) copy-start(f32[4,1,256]{2,1,0:T(1,128)S(1)} %convert_element_type.155) | copy-start | bytes 12292
  53.6 79.2 %copy-start.24 = (f32[4,1,256]{2,1,0:T(1,128)}, f32[4,1,256]{2,1,0:T(1,128)S(1)}, u32[]{:S(2)}) copy-start(f32[4,1,256]{2,1,0:T(1,128)S(1)} %convert_element_type.158) | copy-start | bytes 12292
  90.4 42.5 %copy-start.9 = (bf16[256,1024]{1,0:T(8,128)(2,1)}, bf16[256,1024]{1,0:T(8,128)(2,1)S(1)}, u32[]{:S(2)}) copy-start(bf16[256,1024]{1,0:T(8,128)(2,1)S(1)} %get-tuple-element.594) | copy-start | bytes 1572868
  132.9 1.7 copy-start.13
  135.6 414.5 %all-gather.20.cloned.1.call-start = ((), (), s32[]{:S(2)}) async-start(), calls=%async_computation.4 | async-start | bytes 4718592 | tf_op jit(solution)/shard_map/all_gather | solution.py:170
  135.8 9.0 copy-start.26
  135.8 9.0 copy-start.28
  144.2 6.5 copy-start.39
  148.7 509.0 %all-gather.28.cloned.1.call-start = ((), (), s32[]{:S(2)}) async-start(), calls=%async_computation.8 | async-start | bytes 4718592 | tf_op jit(solution)/shard_map/all_gather | solution.py:261
  150.7 538.0 %all-gather.30.cloned.1.call-start = ((), (), s32[]{:S(2)}) async-start(), calls=%async_computation.9 | async-start | bytes 4718592 | tf_op jit(solution)/shard_map/all_gather | solution.py:262
  177.0 155.2 %copy-start.6 = (bf16[2,128,1024]{2,1,0:T(8,128)(2,1)S(1)}, bf16[2,128,1024]{2,1,0:T(8,128)(2,1)}, u32[]{:S(2)}) copy-start(bf16[2,128,1024]{2,1,0:T(8,128)(2,1)} %param.24) | copy-start | bytes 1572868
  338.7 2.3 copy-start.5
  342.4 466.7 %reduce-scatter.5.cloned.1.call-start = ((), (), s32[]{:S(2)}) async-start(), calls=%async_computation.11 | async-start | bytes 13107200 | tf_op jit(solution)/shard_map/reduce_scatter | solution.py:336
  557.9 5.6 copy-start
  612.0 5.6 copy-start.14
  612.0 446.1 %reduce-scatter.3.cloned.1.call-start = ((), (), s32[]{:S(2)}) async-start(), calls=%async_computation.10 | async-start | bytes 18350080 | tf_op jit(solution)/shard_map/reduce_scatter | solution.py:342
  617.6 7.4 copy-start.11
  617.6 7.4 copy-start.21
  696.7 5.2 copy-start.15
  696.7 5.2 copy-start.19
  701.9 48.9 %copy-start.27 = (f32[128,8]{0,1:T(8,128)S(1)}, f32[128,8]{0,1:T(8,128)}, u32[]{:S(2)}) copy-start(f32[128,8]{0,1:T(8,128)} %copy-done.26) | copy-start | bytes 12292
  701.9 48.9 %copy-start.29 = (f32[128,8]{0,1:T(8,128)S(1)}, f32[128,8]{0,1:T(8,128)}, u32[]{:S(2)}) copy-start(f32[128,8]{0,1:T(8,128)} %copy-done.28) | copy-start | bytes 12292
  750.7 4.1 copy-start.18
  752.8 0.6 copy-start.16
  754.2 1.7 copy-start.10
  754.3 3.5 slice-start
  755.9 1.9 copy-start.12
  755.9 3.0 slice-start.1
  769.4 0.7 copy-start.46
  769.4 12.6 %copy-start.47 = (bf16[256]{0:T(256)(128)(2,1)S(1)}, bf16[256]{0:T(256)(128)(2,1)}, u32[]{:S(2)}) copy-start(bf16[256]{0:T(256)(128)(2,1)} %param.33) | copy-start | bytes 1540
  769.4 22.8 %copy-start.7 = (bf16[2,128,1024]{2,1,0:T(8,128)(2,1)S(1)}, bf16[2,128,1024]{2,1,0:T(8,128)(2,1)}, u32[]{:S(2)}) copy-start(bf16[2,128,1024]{2,1,0:T(8,128)(2,1)} %param.24) | copy-start | bytes 1572868
  769.4 397.8 %all-reduce.6.cloned.1.call-start = ((), (), s32[]{:S(2)}) async-start(), calls=%async_computation.12 | async-start | bytes 12582912 | tf_op jit(solution)/shard_map/psum | solution.py:350
  1058.1 7.6 slice-start.2
  1058.1 7.6 slice-start.3
  1058.1 7.6 slice-start.4
  1058.1 7.6 copy-start.4
  1058.2 7.6 copy-start.20
  1058.2 7.6 copy-start.36
  1058.2 7.6 copy-start.37
  1058.2 8.3 copy-start.49
  1066.5 6.6 copy-start.23
  1066.5 6.6 copy-start.25
  1073.1 7.1 copy-start.30
  1073.1 7.1 copy-start.31
  1073.1 54.1 %copy-start.8 = (bf16[2,128,1024]{2,1,0:T(8,128)(2,1)S(1)}, bf16[2,128,1024]{2,1,0:T(8,128)(2,1)}, u32[]{:S(2)}) copy-start(bf16[2,128,1024]{2,1,0:T(8,128)(2,1)} %param.24) | copy-start | bytes 1572868
  1073.1 54.1 %copy-start.17 = (f32[256,1024]{1,0:T(8,128)S(1)}, f32[256,1024]{1,0:T(8,128)}, u32[]{:S(2)}) copy-start(f32[256,1024]{1,0:T(8,128)} %fusion.159) | copy-start | bytes 3145732
  1073.2 54.1 %copy-start.33 = (f32[256]{0:T(256)S(1)}, f32[256]{0:T(256)}, u32[]{:S(2)}) copy-start(f32[256]{0:T(256)} %copy-done.32) | copy-start | bytes 3076
  1073.2 54.1 %copy-start.35 = (f32[256]{0:T(256)S(1)}, f32[256]{0:T(256)}, u32[]{:S(2)}) copy-start(f32[256]{0:T(256)} %copy-done.34) | copy-start | bytes 3076
  1125.4 57.1 %copy-start.38 = (f32[256]{0:T(256)}, f32[256]{0:T(256)S(1)}, u32[]{:S(2)}) copy-start(f32[256]{0:T(256)S(1)} %dynamic_slice.78) | copy-start | bytes 3076
  1167.2 3.6 copy-start.1
  1170.8 2.5 copy-start.2
  (2 other events, 1.2 us)
Sparse Core Ops, SparseCore 0:
  9.6 118.5 all-gather.15
  129.8 43.9 all-gather.23
  175.4 148.4 all-gather.25
  325.3 147.7 all-gather.21
  475.4 35.5 all-gather.17
  512.7 37.3 all-gather.19
  551.9 37.3 all-gather.27
  591.2 37.3 all-gather.29
  630.9 178.1 reduce-scatter.4
  811.3 246.6 reduce-scatter.2
  1061.5 105.6 all-reduce.5
where the time goes:
time: 1200 us; the launch traced here: 1190 us
  waiting for transfers between devices  685 us (57%)
  blocking collectives  170 us (14%)
  matrix products  158 us (13%)
  local copies, waits for them, and re-layouts  119 us (10%)
  other arithmetic  39.7 us (3%)
  between operations  15.8 us (1%)
    reduce_scatter x1, waiting for transfers between devices, per_device(): lax.psum_scatter(in_term(jnp.int32(0), row_count * lax.axis_size('fsdp'))...  249 us
    all_gather x1, waiting for transfers between devices, per_device(): lax.all_gather(ff_out_weight, 'fsdp', axis=0, tiled=True)  147 us
    all_gather x1, waiting for transfers between devices, per_device(): lax.all_gather(ff_in_weight, 'fsdp', axis=0, tiled=True)  130 us
    unnamed x136, local copies, waits for them, and re-layouts  45.5 us
    psum x1, blocking collectives, per_device(): lax.psum((gain_grad_one, shift_grad_one, gain_grad_two, shift_grad_two, q...  42.5 us
    all_gather x1, waiting for transfers between devices, per_device(): lax.all_gather(qkv_weight, 'fsdp', axis=0, tiled=True)  37.9 us
    psum x1, waiting for transfers between devices, per_device(): lax.psum(in_part.astype(jnp.bfloat16), 'ctx').astype(jnp.float32)  37.1 us
    reshape x4, local copies, waits for them, and re-layouts, blocked(): matrix.reshape(seq_count, blocks, key_block, H, HD).transpose(1, 0, 2, 3, 4)  31.5 us
  transfers between devices with their start and end apart: 11, of which 9 were waited for; matrix products, arithmetic and copies ran while one was open for 25% of the time, Pallas kernels for 0%

commit v1 on v0

--- a/solution.py
+++ b/solution.py
@@ -9,6 +9,17 @@
 HD = 64
 ROT = 16
 EPSILON = 1e-05
+
+
+def gather_around(value, axis, dim):
+    ways = lax.axis_size(axis)
+    pieces = [value]
+    for far in range(1, ways):
+        pieces.append(
+            lax.ppermute(pieces[far - 1], axis, [(d, (d - 1) % ways) for d in range(ways)])
+        )
+    line = jnp.concatenate(pieces, axis=dim)
+    return jnp.roll(line, lax.axis_index(axis) * value.shape[dim], axis=dim)
 
 
 def layer_norm(inputs, gain_vec, shift_vec):
@@ -147,7 +158,7 @@
         lax.all_gather(qkv_weight, "fsdp", axis=0, tiled=True),
         lax.all_gather(ff_in_weight, "fsdp", axis=0, tiled=True),
         lax.all_gather(attn_out_weight, "fsdp", axis=0, tiled=True),
-        lax.all_gather(ff_out_weight, "fsdp", axis=0, tiled=True),
+        gather_around(ff_out_weight, "fsdp", 0),
     )
     query_pos = paired_position(
         jnp.arange(tokens, dtype=jnp.int32) + ctx_place * tokens, half_rows, ctx_count

time: 1200 us -> 1180 us (0.983)
  waiting for transfers between devices: 685 us -> 631 us
  local copies, waits for them, and re-layouts: 119 us -> 144 us
    ppermute x0 -> x3, waiting for transfers between devices: none -> 279 us  [gather_around(): lax.ppermute(pieces[far - 1], axis, [(d, (d - 1) % ways) for d in range(w...]
    all_gather x1 -> x0, waiting for transfers between devices: 147 us -> none  [per_device(): lax.all_gather(ff_out_weight, 'fsdp', axis=0, tiled=True)]
    all_gather x1, waiting for transfers between devices: 130 us -> 0.02 us  [per_device(): lax.all_gather(ff_in_weight, 'fsdp', axis=0, tiled=True)]
    all_gather x1, waiting for transfers between devices: 28.6 us -> 0.01 us  [per_device(): lax.all_gather(values_b, 'ctx', axis=1, tiled=True)]
    all_gather x1, waiting for transfers between devices: 25.9 us -> 8.65 us  [per_device(): lax.all_gather(keys_b.reshape(seq_count, tokens, D), 'ctx', axis=1, tiled...]
    unnamed x136 -> x132, local copies, waits for them, and re-layouts: 45.5 us -> 57.5 us
  transfers between devices with their start and end apart: 11 -> 13, of which waited for: 9 -> 8; matrix products, arithmetic and copies ran while one was open for 25% -> 28% of each run, Pallas kernels for 0% -> 0%
where the time goes in v1:
time: 1180 us; the launch traced here: 1170 us
  waiting for transfers between devices  631 us (53%)
  blocking collectives  169 us (14%)
  matrix products  161 us (14%)
  local copies, waits for them, and re-layouts  144 us (12%)
  other arithmetic  40.8 us (3%)
  between operations  15.9 us (1%)
    ppermute x3, waiting for transfers between devices, gather_around(): lax.ppermute(pieces[far - 1], axis, [(d, (d - 1) % ways) for d in range(w...  279 us
    reduce_scatter x1, waiting for transfers between devices, per_device(): lax.psum_scatter(in_term(jnp.int32(0), row_count * lax.axis_size('fsdp'))...  249 us
    unnamed x132, local copies, waits for them, and re-layouts  57.5 us
    psum x1, blocking collectives, per_device(): lax.psum((gain_grad_one, shift_grad_one, gain_grad_two, shift_grad_two, q...  42.8 us
    all_gather x1, waiting for transfers between devices, per_device(): lax.all_gather(qkv_weight, 'fsdp', axis=0, tiled=True)  38.5 us
    psum x1, waiting for transfers between devices, per_device(): lax.psum(in_part.astype(jnp.bfloat16), 'ctx').astype(jnp.float32)  33.8 us
    reshape x4, local copies, waits for them, and re-layouts, blocked(): matrix.reshape(seq_count, blocks, key_block, H, HD).transpose(1, 0, 2, 3, 4)  31.5 us
    dot_general x4, matrix products, block_scores(): jnp.einsum('sqhd,skhd->shqk', query_b, key_piece, preferred_element_type=...  25.9 us
  transfers between devices with their start and end apart: 13, of which 8 were waited for; matrix products, arithmetic and copies ran while one was open for 28% of the time, Pallas kernels for 0%

profile of v1, /device:TPU:0, one launch (start us, length us, event | category | flops | bytes accessed | tf_op | source)
XLA Modules:
  0.0 1165.7 jit_solution(6973081452045669280)
XLA Ops:
  9.6 12.7 %all-gather.1 = bf16[4,1,256]{2,1,0:T(2,128)(2,1)S(1)} all-gather(bf16[1,1,256]{2,1,0:T(2,128)(2,1)S(1)} %reshape.446), channel_id=1, replica_groups=mesh['ctx'=8,'fsdp'=4] {'fsdp'}, dimensions={0}, use_global_device_ids=true | all-gather | bytes 2560 | tf_op jit(solution)/shard_map/all_gather | solution.py:133
  22.2 8.1 all-gather
  30.4 14.8 %all-gather.4 = bf16[4,1,256]{2,1,0:T(2,128)(2,1)S(1)} all-gather(bf16[1,1,256]{2,1,0:T(2,128)(2,1)S(1)} %reshape.452), channel_id=1, replica_groups=mesh['ctx'=8,'fsdp'=4] {'fsdp'}, dimensions={0}, use_global_device_ids=true | all-gather | bytes 2560 | tf_op jit(solution)/shard_map/all_gather | solution.py:135
  45.2 8.4 all-gather.3
  55.2 15.9 %all-reduce.1 = bf16[256]{0:T(256)(128)(2,1)S(1)} all-reduce(bf16[256]{0:T(256)(128)(2,1)S(1)} %dynamic-update-slice), channel_id=1, replica_groups=mesh['ctx'=8,'fsdp'=4] {'fsdp'}, use_global_device_ids=true, to_apply=%add.1 | all-reduce | flops 256 | bytes 1024
  71.3 16.8 %all-gather.2 = bf16[4,1,512]{2,1,0:T(2,128)(2,1)S(1)} all-gather(bf16[1,1,512]{2,1,0:T(2,128)(2,1)S(1)} %reshape.448), channel_id=1, replica_groups=mesh['ctx'=8,'fsdp'=4] {'fsdp'}, dimensions={0}, use_global_device_ids=true | all-gather | bytes 5120 | tf_op jit(solution)/shard_map/all_gather | solution.py:136
  89.8 38.5 %all-gather.15.cloned.1.call-done = bf16[1024,3072]{1,0:T(8,128)(2,1)} async-done(((bf16[256,3072]{1,0:T(8,128)(2,1)}), bf16[1024,3072]{1,0:T(8,128)(2,1)}) %all-gather.15.cloned.1.call-update) | async-done | bytes 6291472 | tf_op jit(solution)/shard_map/all_gather | solution.py:158
  128.3 4.7 convolution_add_fusion.1
  136.1 81.1 %collective-permute-done = bf16[256,4096]{1,0:T(8,128)(2,1)} collective-permute-done((bf16[256,4096]{1,0:T(8,128)(2,1)S(1)}, bf16[256,4096]{1,0:T(8,128)(2,1)}, u32[]{:S(2)}, u32[]{:S(2)}) %collective-permute-start) | collective-permute-done | bytes 2097184 | tf_op jit(solution)/shard_map/ppermute | solution.py:19
  238.6 104.2 %collective-permute-done.1 = bf16[256,4096]{1,0:T(8,128)(2,1)} collective-permute-done((bf16[256,4096]{1,0:T(8,128)(2,1)}, bf16[256,4096]{1,0:T(8,128)(2,1)}, u32[]{:S(2)}, u32[]{:S(2)}) %collective-permute-start.1) | collective-permute-done | bytes 2097184 | tf_op jit(solution)/shard_map/ppermute | solution.py:19
  347.5 3.2 constant_dynamic-update-slice_fusion.5
  350.7 93.9 %collective-permute-done.2 = bf16[256,4096]{1,0:T(8,128)(2,1)} collective-permute-done((bf16[256,4096]{1,0:T(8,128)(2,1)}, bf16[256,4096]{1,0:T(8,128)(2,1)}, u32[]{:S(2)}, u32[]{:S(2)}) %collective-permute-start.2) | collective-permute-done | bytes 2097184 | tf_op jit(solution)/shard_map/ppermute | solution.py:19
  444.5 3.2 constant_dynamic-update-slice_fusion.4
  455.5 3.3 constant_dynamic-update-slice_fusion
  458.8 7.8 constant_dynamic-slice_fusion.6
  466.6 6.3 convolution_bitcast_fusion
  476.5 12.4 %all_gather.64 = bf16[4096]{0:T(1024)(128)(2,1)S(1)} all-gather(bf16[1024]{0:T(1024)(128)(2,1)S(1)} %copy-done.37), channel_id=1, replica_groups=mesh['ctx'=8,'fsdp'=4] {'fsdp'}, dimensions={0}, use_global_device_ids=true | all-gather | bytes 10240 | tf_op jit(solution)/shard_map/all_gather | solution.py:139
  494.3 9.6 fusion.191
  503.9 7.9 reshape.422
  511.8 5.2 copy.89
  516.9 8.6 all-gather.19.cloned.1.call-done
  525.6 7.8 reshape.424
  533.4 5.5 copy.90
  538.9 24.1 %while.48 = (s32[]{:T(128)}, f32[2,16,128]{2,1,0:T(8,128)S(1)}, f32[2,16,128]{2,1,0:T(8,128)S(1)}, s32[2,512]{1,0:T(2,128)S(1)}, bf16[2,2,512,16,64]{2,4,3,1,0:T...) while((s32[]{:T(128)}, f32[2,16,128]{2,1,0:T(8,128)S(1)}, ...), condition=%wide.region_5.6_spmd.clone, body=%wide.region_2.5_spmd.clone.sunk | while | flops 283205120 | bytes 19815548 | solution.py:214
  539.1 6.6 fusion.245
  545.7 5.2 exponential_reduce_fusion.2
  551.2 6.6 fusion.245
  557.8 5.2 exponential_reduce_fusion.2
  563.1 13.2 %while.49 = (s32[]{:T(128)}, f32[2,128,16,64]{1,3,2,0:T(8,128)}, bf16[2,2,512,16,64]{2,4,3,1,0:T(8,128)(2,1)}, s32[2,512]{1,0:T(2,128)S(1)}, bf16[2,2,512,16,64]...) while((s32[]{:T(128)}, f32[2,128,16,64]{1,3,2,0:T(8,128)}, ...), condition=%wide.region_7.8_spmd.clone, body=%wide.region_6.7_spmd.clone.sunk | while | flops 547950080 | bytes 6972030 | solution.py:228
  563.3 6.2 fusion.251
  569.6 6.4 fusion.251
  581.6 7.4 convert_bitcast_fusion
  591.8 7.4 convolution_convert_fusion
  599.2 8.0 reshape.432
  607.2 5.3 copy.112
  612.5 30.9 %while.50 = (s32[]{:T(128)}, f32[2,128,16,64]{1,3,2,0:T(8,128)S(1)}, bf16[2,2,512,16,64]{2,4,3,1,0:T(8,128)(2,1)}, s32[2,512]{1,0:T(2,128)S(1)}, bf16[2,128,16,6...) while((s32[]{:T(128)}, ...), condition=%wide.region_10.11_spmd.clone, body=%wide.region_9.10_spmd.clone.sunk | while | flops 820841984 | bytes 26387088 | solution.py:270
  612.5 6.5 fusion.258
  619.1 8.9 fusion.259
  628.0 6.2 fusion.258
  634.4 8.9 fusion.259
  645.2 7.8 reshape.430
  653.0 5.3 copy.109
  658.2 9.4 all_gather.69
  667.8 8.2 all_gather.71
  676.2 48.3 %while.51 = (s32[]{:T(128)}, f32[2,128,16,64]{1,3,2,0:T(8,128)S(1)}, f32[2,128,16,64]{1,3,2,0:T(8,128)}, bf16[2,2,512,16,64]{2,4,3,1,0:T(8,128)(2,1)}, s32[2,512...) while((s32[]{:T(128)}, ...), condition=%wide.region_12.13_spmd.clone, body=%wide.region_11.12_spmd.clone.sunk | while | flops 1100287488 | bytes 39723684 | solution.py:313
  676.4 6.2 fusion.267
  682.9 11.0 fusion.268
  693.9 6.3 fusion.269
  700.2 6.3 fusion.267
  706.9 10.7 fusion.268
  717.6 6.5 fusion.269
  732.3 10.5 pad_maximum_fusion
  743.4 11.4 all-gather.6
  755.4 8.1 all-gather.5
  764.8 19.7 %reduce-scatter.5.cloned.1.call-done = bf16[256,5120]{0,1:T(8,128)(2,1)} async-done(((bf16[1024,5120]{0,1:T(8,128)(2,1)}), bf16[256,5120]{0,1:T(8,128)(2,1)}) %reduce-scatter.5.cloned.1.call-update) | async-done | bytes 2621456 | tf_op jit(solution)/shard_map/reduce_scatter | solution.py:347
  784.5 249.2 %reduce-scatter.3.cloned.1.call-done = bf16[256,7168]{1,0:T(8,128)(2,1)} async-done(((bf16[1024,7168]{1,0:T(8,128)(2,1)}), bf16[256,7168]{1,0:T(8,128)(2,1)}) %reduce-scatter.3.cloned.1.call-update) | async-done | bytes 3670032 | tf_op jit(solution)/shard_map/reduce_scatter | solution.py:353
  1033.7 7.4 fusion.182
  1045.4 6.3 fusion.176
  1051.7 42.8 %all-reduce.2 = (f32[1024]{0:T(1024)S(1)}, f32[1024]{0:T(1024)S(1)}, f32[1024]{0:T(1024)S(1)}, f32[1024]{0:T(1024)S(1)}, f32[2048]{0:T(1024)S(1)}, /*index=5*/f3...) all-reduce(f32[1024]{0:T(1024)S(1)} %get-tuple-element.477, ...), channel_id=1, replica_groups=mesh['ctx'=8,'fsdp'=4] {'ctx','fsdp'}, use_global_device_ids=true, to_apply=%region_18.19 | all-reduce | flops 11520 | bytes 92160 | tf_op jit(solution)/shard_map/psum | solution.py:367
  1098.9 3.2 fusion.172
  1102.2 6.8 fusion.180
  1108.9 33.8 %all-reduce.6.cloned.1.call-done = (bf16[256,7168]{1,0:T(8,128)(2,1)}, bf16[256,5120]{0,1:T(8,128)(2,1)}) async-done(((bf16[256,7168]{1,0:T(8,128)(2,1)}, bf16[256,5120]{0,1:T(8,128)(2,1)}), (bf16[256,7168]{1,0:T(8,128)(2,1)}, bf16[256,5120]{0,1:T(8,128)(2,1)})) %all-reduce.6.cloned.1.call-update) | async-done | bytes 6291472 | tf_op jit(solution)/shard_map/psum | solution.py:361
  1142.7 3.6 slice.117
  1152.5 5.6 copy.122
  (277 shorter events, 88.0 us)
Async XLA Ops:
  7.2 46.5 %copy-start.47 = (u32[32]{0:T(128)S(1)}, u32[32]{0:T(128)}, u32[]{:S(2)}) copy-start(u32[32]{0:T(128)} %constant.205) | copy-start | bytes 388
  7.2 2.3 copy-start.40
  7.2 15.0 %copy-start.41 = (bf16[256]{0:T(256)(128)(2,1)S(1)}, bf16[256]{0:T(256)(128)(2,1)}, u32[]{:S(2)}) copy-start(bf16[256]{0:T(256)(128)(2,1)} %param.25) | copy-start | bytes 1540
  7.2 23.1 %copy-start.42 = (bf16[256]{0:T(256)(128)(2,1)S(1)}, bf16[256]{0:T(256)(128)(2,1)}, u32[]{:S(2)}) copy-start(bf16[256]{0:T(256)(128)(2,1)} %param.28) | copy-start | bytes 1540
  7.2 38.0 %copy-start.43 = (bf16[256]{0:T(256)(128)(2,1)S(1)}, bf16[256]{0:T(256)(128)(2,1)}, u32[]{:S(2)}) copy-start(bf16[256]{0:T(256)(128)(2,1)} %param.27) | copy-start | bytes 1540
  7.2 46.4 %copy-start.38 = (bf16[512]{0:T(512)(128)(2,1)S(1)}, bf16[512]{0:T(512)(128)(2,1)}, u32[]{:S(2)}) copy-start(bf16[512]{0:T(512)(128)(2,1)} %param.30) | copy-start | bytes 3076
  7.2 47.7 %copy-start.44 = (bf16[64]{0:T(256)(128)(2,1)S(1)}, bf16[64]{0:T(256)(128)(2,1)}, u32[]{:S(2)}) copy-start(bf16[64]{0:T(256)(128)(2,1)} %param.31) | copy-start | bytes 388
  7.3 80.9 %copy-start.3 = (bf16[2,128,1024]{2,1,0:T(8,128)(2,1)S(1)}, bf16[2,128,1024]{2,1,0:T(8,128)(2,1)}, u32[]{:S(2)}) copy-start(bf16[2,128,1024]{2,1,0:T(8,128)(2,1)} %param.23) | copy-start | bytes 1572868
  7.3 121.0 %all-gather.15.cloned.1.call-start = ((), (), s32[]{:S(2)}) async-start(), calls=%async_computation.2 | async-start | bytes 7864320 | tf_op jit(solution)/shard_map/all_gather | solution.py:158
  8.0 458.6 %all-gather.23.cloned.1.call-start = ((), (), s32[]{:S(2)}) async-start(), calls=%async_computation.6 | async-start | bytes 2621440 | tf_op jit(solution)/shard_map/all_gather | solution.py:160
  8.8 485.5 %all-gather.21.cloned.1.call-start = ((), (), s32[]{:S(2)}) async-start(), calls=%async_computation.5 | async-start | bytes 10485760 | tf_op jit(solution)/shard_map/all_gather | solution.py:159
  9.5 494.4 %all-gather.17.cloned.1.call-start = ((), (), s32[]{:S(2)}) async-start(), calls=%async_computation.3 | async-start | bytes 4718592 | tf_op jit(solution)/shard_map/all_gather | solution.py:182
  30.3 97.9 %copy-start.20 = (f32[4,1,256]{2,1,0:T(1,128)}, f32[4,1,256]{2,1,0:T(1,128)S(1)}, u32[]{:S(2)}) copy-start(f32[4,1,256]{2,1,0:T(1,128)S(1)} %convert_element_type.155) | copy-start | bytes 12292
  53.7 74.6 %copy-start.22 = (f32[4,1,256]{2,1,0:T(1,128)}, f32[4,1,256]{2,1,0:T(1,128)S(1)}, u32[]{:S(2)}) copy-start(f32[4,1,256]{2,1,0:T(1,128)S(1)} %convert_element_type.158) | copy-start | bytes 12292
  88.3 40.0 %copy-start.30 = (f32[256]{0:T(256)}, f32[256]{0:T(256)S(1)}, u32[]{:S(2)}) copy-start(f32[256]{0:T(256)S(1)} %get-tuple-element.604) | copy-start | bytes 3076
  88.6 39.7 %copy-start.32 = (f32[256]{0:T(256)}, f32[256]{0:T(256)S(1)}, u32[]{:S(2)}) copy-start(f32[256]{0:T(256)S(1)} %rsqrt_bitcast_fusion) | copy-start | bytes 3076
  89.8 38.5 %copy-start.6 = (bf16[256,1024]{1,0:T(8,128)(2,1)}, bf16[256,1024]{1,0:T(8,128)(2,1)S(1)}, u32[]{:S(2)}) copy-start(bf16[256,1024]{1,0:T(8,128)(2,1)S(1)} %get-tuple-element.594) | copy-start | bytes 1572868
  128.3 7.6 copy-start.5
  133.0 1.7 copy-start.9
  135.8 389.8 %all-gather.19.cloned.1.call-start = ((), (), s32[]{:S(2)}) async-start(), calls=%async_computation.4 | async-start | bytes 4718592 | tf_op jit(solution)/shard_map/all_gather | solution.py:181
  135.8 81.3 %collective-permute-start = (bf16[256,4096]{1,0:T(8,128)(2,1)S(1)}, bf16[256,4096]{1,0:T(8,128)(2,1)}, u32[]{:S(2)}, u32[]{:S(2)}) collective-permute-start(bf16[256,4096]{1,0:T(8,128)(2,1)S(1)} %copy-done.5), channel_id=1, source_target_pairs={{0,3},{1,0},{2,1},{3,2},{4,7},{5,4},{6,5},{7,6},{8,11},{9,8},{10,9... | collective-permute-start | bytes 6291464 | tf_op jit(solution)/shard_map/ppermute | solution.py:19
  217.1 125.7 %collective-permute-start.1 = (bf16[256,4096]{1,0:T(8,128)(2,1)}, bf16[256,4096]{1,0:T(8,128)(2,1)}, u32[]{:S(2)}, u32[]{:S(2)}) collective-permute-start(bf16[256,4096]{1,0:T(8,128)(2,1)} %collective-permute-done), channel_id=1, source_target_pairs={{0,3},{1,0},{2,1},{3,2},{4,7},{5,4},{6,5},{7,6},{8,11},{9,8},{10,9... | collective-permute-start | bytes 6291464 | tf_op jit(solution)/shard_map/ppermute | solution.py:19
  219.4 15.5 %copy-start.24 = (f32[128,8]{0,1:T(8,128)}, f32[128,8]{0,1:T(8,128)S(1)}, u32[]{:S(2)}) copy-start(f32[128,8]{0,1:T(8,128)S(1)} %get-tuple-element.602) | copy-start | bytes 12292
  219.4 15.5 %copy-start.26 = (f32[128,8]{0,1:T(8,128)}, f32[128,8]{0,1:T(8,128)S(1)}, u32[]{:S(2)}) copy-start(f32[128,8]{0,1:T(8,128)S(1)} %get-tuple-element.603) | copy-start | bytes 12292
  238.6 360.6 %all-gather.27.cloned.1.call-start = ((), (), s32[]{:S(2)}) async-start(), calls=%async_computation.8 | async-start | bytes 4718592 | tf_op jit(solution)/shard_map/all_gather | solution.py:273
  342.8 101.7 %collective-permute-start.2 = (bf16[256,4096]{1,0:T(8,128)(2,1)}, bf16[256,4096]{1,0:T(8,128)(2,1)}, u32[]{:S(2)}, u32[]{:S(2)}) collective-permute-start(bf16[256,4096]{1,0:T(8,128)(2,1)} %collective-permute-done.1), channel_id=1, source_target_pairs={{0,3},{1,0},{2,1},{3,2},{4,7},{5,4},{6,5},{7,6},{8,11},{9,8},{10,9... | collective-permute-start | bytes 6291464 | tf_op jit(solution)/shard_map/ppermute | solution.py:19
  458.8 7.8 copy-start.10
  466.6 9.9 copy-start.37
  472.9 2.4 copy-start.19
  475.3 17.2 %copy-start.17 = (bf16[2,128,16,8]{1,0,3,2:T(2,128)(2,1)S(1)}, bf16[2,128,16,8]{1,0,3,2:T(2,128)(2,1)}, u32[]{:S(2)}) copy-start(bf16[2,128,16,8]{1,0,3,2:T(2,128)(2,1)} %get-tuple-element.588) | copy-start | bytes 196612
  475.3 17.2 %copy-start.18 = (bf16[2,128,16,8]{1,0,3,2:T(2,128)(2,1)S(1)}, bf16[2,128,16,8]{1,0,3,2:T(2,128)(2,1)}, u32[]{:S(2)}) copy-start(bf16[2,128,16,8]{1,0,3,2:T(2,128)(2,1)} %get-tuple-element.589) | copy-start | bytes 196612
  476.4 168.7 %all-gather.25.cloned.1.call-start = ((), (), s32[]{:S(2)}) async-start(), calls=%async_computation.7 | async-start | bytes 4718592 | tf_op jit(solution)/shard_map/all_gather | solution.py:272
  494.2 290.3 %reduce-scatter.5.cloned.1.call-start = ((), (), s32[]{:S(2)}) async-start(), calls=%async_computation.10 | async-start | bytes 13107200 | tf_op jit(solution)/shard_map/reduce_scatter | solution.py:347
  533.4 5.5 copy-start
  589.1 444.6 %reduce-scatter.3.cloned.1.call-start = ((), (), s32[]{:S(2)}) async-start(), calls=%async_computation.9 | async-start | bytes 18350080 | tf_op jit(solution)/shard_map/reduce_scatter | solution.py:353
  607.2 5.3 copy-start.8
  607.2 5.3 copy-start.16
  653.0 23.2 %copy-start.12 = (f32[2,128,16,64]{1,3,2,0:T(8,128)S(1)}, f32[2,128,16,64]{1,3,2,0:T(8,128)}, u32[]{:S(2)}) copy-start(f32[2,128,16,64]{1,3,2,0:T(8,128)} %custom-call.4) | copy-start | bytes 3145732
  676.2 49.3 %copy-start.25 = (f32[128,8]{0,1:T(8,128)S(1)}, f32[128,8]{0,1:T(8,128)}, u32[]{:S(2)}) copy-start(f32[128,8]{0,1:T(8,128)} %copy-done.24) | copy-start | bytes 12292
  676.2 49.3 %copy-start.27 = (f32[128,8]{0,1:T(8,128)S(1)}, f32[128,8]{0,1:T(8,128)}, u32[]{:S(2)}) copy-start(f32[128,8]{0,1:T(8,128)} %copy-done.26) | copy-start | bytes 12292
  725.3 3.5 copy-start.14
  727.5 2.2 copy-start.13
  728.2 1.8 copy-start.7
  728.3 3.5 slice-start
  729.9 2.3 slice-start.1
  742.8 0.7 copy-start.45
  742.8 12.6 %copy-start.46 = (bf16[256]{0:T(256)(128)(2,1)S(1)}, bf16[256]{0:T(256)(128)(2,1)}, u32[]{:S(2)}) copy-start(bf16[256]{0:T(256)(128)(2,1)} %param.33) | copy-start | bytes 1540
  742.8 21.4 %copy-start.11 = (bf16[2,128,1024]{2,1,0:T(8,128)(2,1)S(1)}, bf16[2,128,1024]{2,1,0:T(8,128)(2,1)}, u32[]{:S(2)}) copy-start(bf16[2,128,1024]{2,1,0:T(8,128)(2,1)} %param.24) | copy-start | bytes 1572868
  742.8 399.9 %all-reduce.6.cloned.1.call-start = ((), (), s32[]{:S(2)}) async-start(), calls=%async_computation.11 | async-start | bytes 12582912 | tf_op jit(solution)/shard_map/psum | solution.py:361
  1033.7 11.7 %copy-start.4 = (bf16[2,128,1024]{2,1,0:T(8,128)(2,1)S(1)}, bf16[2,128,1024]{2,1,0:T(8,128)(2,1)}, u32[]{:S(2)}) copy-start(bf16[2,128,1024]{2,1,0:T(8,128)(2,1)} %param.23) | copy-start | bytes 1572868
  1033.7 11.7 %copy-start.21 = (f32[4,1,256]{2,1,0:T(1,128)S(1)}, f32[4,1,256]{2,1,0:T(1,128)}, u32[]{:S(2)}) copy-start(f32[4,1,256]{2,1,0:T(1,128)} %copy-done.20) | copy-start | bytes 12292
  1033.7 11.6 copy-start.23
  1045.3 6.3 copy-start.28
  1045.4 6.3 copy-start.29
  1045.4 53.6 %copy-start.31 = (f32[256]{0:T(256)S(1)}, f32[256]{0:T(256)}, u32[]{:S(2)}) copy-start(f32[256]{0:T(256)} %copy-done.30) | copy-start | bytes 3076
  1045.4 53.6 %copy-start.33 = (f32[256]{0:T(256)S(1)}, f32[256]{0:T(256)}, u32[]{:S(2)}) copy-start(f32[256]{0:T(256)} %copy-done.32) | copy-start | bytes 3076
  1051.7 50.5 %copy-start.15 = (bf16[256,1024]{1,0:T(8,128)(2,1)S(1)}, bf16[256,1024]{1,0:T(8,128)(2,1)}, u32[]{:S(2)}) copy-start(bf16[256,1024]{1,0:T(8,128)(2,1)} %copy.93) | copy-start | bytes 1572868
  1051.7 50.5 %copy-start.34 = (f32[4,1,256]{2,1,0:T(1,128)S(1)}, f32[4,1,256]{2,1,0:T(1,128)}, u32[]{:S(2)}) copy-start(f32[4,1,256]{2,1,0:T(1,128)} %convert_element_type.161) | copy-start | bytes 12292
  1051.7 50.5 %copy-start.35 = (f32[4,1,256]{2,1,0:T(1,128)S(1)}, f32[4,1,256]{2,1,0:T(1,128)}, u32[]{:S(2)}) copy-start(f32[4,1,256]{2,1,0:T(1,128)} %convert_element_type.160) | copy-start | bytes 12292
  1094.5 7.7 copy-start.39
  1097.1 61.0 %copy-start.36 = (f32[256]{0:T(256)}, f32[256]{0:T(256)S(1)}, u32[]{:S(2)}) copy-start(f32[256]{0:T(256)S(1)} %dynamic_slice.83) | copy-start | bytes 3076
  1142.7 3.6 copy-start.1
  1146.3 2.5 copy-start.2
Sparse Core Ops, SparseCore 0:
  9.6 118.5 all-gather.14
  129.8 73.7 all-gather.22
  205.2 239.3 all-gather.20
  446.9 39.4 all-gather.16
  488.1 37.4 all-gather.18
  527.3 37.3 all-gather.26
  566.6 37.3 all-gather.24
  606.3 178.1 reduce-scatter.4
  786.8 246.7 reduce-scatter.2
  1036.9 105.8 all-reduce.5
